TPU v7x, 128 devices: a whole 4x4x4 slice. The times are simulated.
128 devices in a mesh: pipe: 2 (over core), tensor: 2 (over x_lo), dp: 32 (over y, z, x_hi).
Axes of the slice: x: 4 (x_hi: 2, x_lo: 2; x = x_hi * 2 + x_lo), y: 4, z: 4, core: 2. Of those that a mesh axis runs over, the one named last changes fastest.
Arguments:
- section_in: bfloat16 [2, 32, 2, 128, 1024], P('pipe', 'dp', 'tensor'), may hold values from -12 to 12
- lengths: int32 [32, 2], P('dp'), may hold values from 32 to 128, as said below
- qkv_weight: bfloat16 [2, 3, 1024, 1024], P('pipe', None, None, 'tensor'), may hold values from -0.75 to 0.75
- qv_bias: bfloat16 [2, 2, 1024], P('pipe', None, 'tensor'), may hold values from -3 to 3
- out_weight: bfloat16 [2, 1024, 1024], P('pipe', 'tensor'), may hold values from -0.5 to 0.5
- up_weight: bfloat16 [2, 1024, 2048], P('pipe', None, 'tensor'), may hold values from -0.1875 to 0.1875
- up_bias: bfloat16 [2, 2048], P('pipe', 'tensor'), may hold values from -3 to 3
- down_weight: bfloat16 [2, 2048, 1024], P('pipe', 'tensor'), may hold values from -0.125 to 0.125
- norm_gains: float32 [2, 2, 1024], P('pipe'), may hold values from 0.5 to 1.5
- row_biases: float32 [2, 4, 1024], P('pipe'), may hold values from -2 to 2
Outputs:
- section_out: float32 [2, 32, 2, 128, 1024], P('pipe', 'dp', 'tensor')
- qkv_grad: float32 [2, 3, 1024, 1024], P('pipe', None, None, 'tensor')
- qv_bias_grad: float32 [2, 2, 1024], P('pipe', None, 'tensor')
- out_grad: float32 [2, 1024, 1024], P('pipe', 'tensor')
- up_grad: float32 [2, 1024, 2048], P('pipe', None, 'tensor')
- up_bias_grad: float32 [2, 2048], P('pipe', 'tensor')
- down_grad: float32 [2, 2048, 1024], P('pipe', 'tensor')
- gain_grad: float32 [2, 2, 1024], P('pipe')
- bias_grad: float32 [2, 4, 1024], P('pipe')
Inputs may be any that keep to these rules, and one draw needn't show every extreme that they name: `lengths`: some sequence has length exactly 128 and some exactly 32.
All inputs are finite; a program needn't handle non-finite values.
Results may differ from a plain program's by a relative error of at most 0.023.
Values may be sent and summed in bfloat16 or wider, within the bound.
No kernel may reach another device: no remote copies, remote signals or barrier semaphores. Data moves between devices by JAX's collectives and lax.ppermute only.
A program may use at most 128 MiB of HBM per device.

v0:
```python
import jax
import jax.numpy as jnp
from jax import lax
from jax.sharding import PartitionSpec as P

HEADS = 16
HD = 64
norm_eps = 1e-05


def shifted(value, axis, steps):
    count = lax.axis_size(axis)
    initial, last = (max(0, -steps), min(count, count - steps))
    return lax.ppermute(value, axis, [(source, source + steps) for source in range(initial, last)])


def gelu_tanh(pre_act):
    return (
        0.5
        * pre_act
        * (1.0 + jnp.tanh(0.7978845608028654 * (pre_act + 0.044715 * pre_act * pre_act * pre_act)))
    )


def norm_fwd(values, gain, shift):
    centred = values - jnp.mean(values, axis=-1, keepdims=True)
    inv_std = lax.rsqrt(jnp.mean(centred * centred, axis=-1, keepdims=True) + norm_eps)
    normed = centred * inv_std
    return (normed * gain + shift, normed, inv_std)


def norm_back(grad_norm, normed, inv_std, gain):
    scaled = grad_norm * gain
    return inv_std * (
        scaled
        - jnp.mean(scaled, axis=-1, keepdims=True)
        - normed * jnp.mean(scaled * normed, axis=-1, keepdims=True)
    )


def rows_product(source, weight, form):
    return jnp.einsum(form, source, weight, preferred_element_type=jnp.float32)


def local(
    section_in,
    lengths,
    qkv_weight,
    qv_bias,
    out_weight,
    up_weight,
    up_bias,
    down_weight,
    norm_gains,
    row_biases,
):
    section_index = lax.axis_index("pipe")
    tensor_index = lax.axis_index("tensor")
    tensor_size = lax.axis_size("tensor")
    groups = section_in.shape[1]
    seq_len = section_in.shape[3]
    model_width = section_in.shape[4]
    total_rows = tensor_size * seq_len
    qkv_w = qkv_weight[0]
    qv_b = qv_bias[0]
    out_w = out_weight[0]
    up_w = up_weight[0]
    up_b = up_bias[0].astype(jnp.float32)
    down_w = down_weight[0]
    gains = norm_gains[0]
    shifts = row_biases[0]
    local_width = qkv_w.shape[2]
    heads_dev = local_width // HD
    head_ids = tensor_index * heads_dev + jnp.arange(heads_dev) + 1
    slopes = 2.0 ** (-8.0 * head_ids.astype(jnp.float32) / HEADS)
    offsets = (jnp.arange(seq_len)[:, None] - jnp.arange(seq_len)[None, :]).astype(jnp.float32)
    key_pos = jnp.arange(seq_len)
    bias_three = jnp.stack([qv_b[0], jnp.zeros_like(qv_b[0]), qv_b[1]]).astype(jnp.float32)[
        :, None, :
    ]
    inputs_all = section_in[0, :, 0]

    def split_heads(block):
        return block.reshape(tensor_size, seq_len, heads_dev, HD)

    def masked_scores(projected, seq_lengths):
        scores = (
            jnp.einsum(
                "bqhd,bkhd->bhqk",
                split_heads(projected[0]),
                split_heads(projected[1]),
                preferred_element_type=jnp.float32,
            )
            * 0.125
            - slopes[None, :, None, None] * offsets
        )
        allowed = (offsets >= 0)[None, None] & (
            key_pos[None, None, None, :] < seq_lengths[:, None, None, None]
        )
        return jnp.where(allowed, scores, -jnp.inf)

    def layer_forward(layer_in, seq_lengths):
        layer_wide = layer_in.astype(jnp.float32)
        attn_f, _, _ = norm_fwd(layer_wide, gains[0], shifts[0])
        attn_full = lax.all_gather(attn_f.astype(jnp.bfloat16), "tensor", axis=0, tiled=True)
        projected = (
            jnp.einsum("rd,cdw->crw", attn_full, qkv_w, preferred_element_type=jnp.float32)
            + bias_three
        ).astype(jnp.bfloat16)
        scores = masked_scores(projected, seq_lengths)
        top_score = jnp.max(scores, axis=-1, keepdims=True)
        exp_scores = jnp.exp(scores - top_score)
        totals = jnp.sum(exp_scores, axis=-1, keepdims=True)
        att_prob = (exp_scores / totals).astype(jnp.bfloat16)
        log_total = top_score + jnp.log(totals)
        context = (
            jnp.einsum(
                "bhqk,bkhd->bqhd",
                att_prob,
                split_heads(projected[2]),
                preferred_element_type=jnp.float32,
            )
            .reshape(total_rows, local_width)
            .astype(jnp.bfloat16)
        )
        attn_out = lax.psum_scatter(
            rows_product(context, out_w, "rw,wd->rd"), "tensor", scatter_dimension=0, tiled=True
        )
        residual = layer_wide + attn_out + shifts[1]
        mlp_f, _, _ = norm_fwd(residual, gains[1], shifts[2])
        mlp_full = lax.all_gather(mlp_f.astype(jnp.bfloat16), "tensor", axis=0, tiled=True)
        pre_gelu = jnp.dot(mlp_full, up_w, preferred_element_type=jnp.float32) + up_b
        activated = gelu_tanh(pre_gelu).astype(jnp.bfloat16)
        mlp_out = lax.psum_scatter(
            rows_product(activated, down_w, "rf,fd->rd"), "tensor", scatter_dimension=0, tiled=True
        )
        layer_out = residual + mlp_out + shifts[3]
        saved = (layer_in, projected, log_total, context, residual, pre_gelu, activated)
        return (layer_out, saved)

    def layer_backward(grad_out, saved, seq_lengths):
        layer_in, projected, log_total, context, residual, pre_gelu, activated = saved[:7]
        attn_f, attn_norm, attn_inv = norm_fwd(layer_in.astype(jnp.float32), gains[0], shifts[0])
        mlp_f, mlp_norm, mlp_inv = norm_fwd(residual, gains[1], shifts[2])
        mlp_full = lax.all_gather(mlp_f.astype(jnp.bfloat16), "tensor", axis=0, tiled=True)
        attn_full = lax.all_gather(attn_f.astype(jnp.bfloat16), "tensor", axis=0, tiled=True)
        grad_full = lax.all_gather(grad_out.astype(jnp.bfloat16), "tensor", axis=0, tiled=True)
        grad_down = jnp.einsum(
            "rf,rd->fd", activated, grad_full, preferred_element_type=jnp.float32
        )
        grad_act = jnp.einsum("rd,fd->rf", grad_full, down_w, preferred_element_type=jnp.float32)
        _, pull_back = jax.vjp(gelu_tanh, pre_gelu)
        grad_pre = pull_back(grad_act)[0]
        grad_pre_half = grad_pre.astype(jnp.bfloat16)
        grad_up = jnp.einsum(
            "rd,rf->df", mlp_full, grad_pre_half, preferred_element_type=jnp.float32
        )
        grad_mlp = lax.psum_scatter(
            rows_product(grad_pre_half, up_w, "rf,df->rd"),
            "tensor",
            scatter_dimension=0,
            tiled=True,
        )
        grad_resid = grad_out + norm_back(grad_mlp, mlp_norm, mlp_inv, gains[1])
        resid_full = lax.all_gather(grad_resid.astype(jnp.bfloat16), "tensor", axis=0, tiled=True)
        grad_outw = jnp.einsum("rw,rd->wd", context, resid_full, preferred_element_type=jnp.float32)
        grad_context = split_heads(
            jnp.einsum("rd,wd->rw", resid_full, out_w, preferred_element_type=jnp.float32).astype(
                jnp.bfloat16
            )
        )
        queries = split_heads(projected[0])
        keys_all = split_heads(projected[1])
        values_all = split_heads(projected[2])
        att_prob = jnp.exp(masked_scores(projected, seq_lengths) - log_total)
        grad_prob = jnp.einsum(
            "bqhd,bkhd->bhqk", grad_context, values_all, preferred_element_type=jnp.float32
        )
        grad_values = jnp.einsum(
            "bhqk,bqhd->bkhd",
            att_prob.astype(jnp.bfloat16),
            grad_context,
            preferred_element_type=jnp.float32,
        )
        row_delta = jnp.sum(att_prob * grad_prob, axis=-1, keepdims=True)
        grad_scores = (att_prob * (grad_prob - row_delta) * 0.125).astype(jnp.bfloat16)
        grad_queries = jnp.einsum(
            "bhqk,bkhd->bqhd", grad_scores, keys_all, preferred_element_type=jnp.float32
        )
        grad_keys = jnp.einsum(
            "bhqk,bqhd->bkhd", grad_scores, queries, preferred_element_type=jnp.float32
        )
        grad_proj = jnp.stack([grad_queries, grad_keys, grad_values]).reshape(
            3, total_rows, local_width
        )
        grad_bias = jnp.stack([jnp.sum(grad_proj[0], axis=0), jnp.sum(grad_proj[2], axis=0)])
        proj_half = grad_proj.astype(jnp.bfloat16)
        grad_qkv = jnp.einsum(
            "rd,crw->cdw", attn_full, proj_half, preferred_element_type=jnp.float32
        )
        grad_attn = lax.psum_scatter(
            rows_product(proj_half, qkv_w, "crw,cdw->rd"), "tensor", scatter_dimension=0, tiled=True
        )
        grad_in = grad_resid + norm_back(grad_attn, attn_norm, attn_inv, gains[0])
        grad_gains = jnp.stack(
            [jnp.sum(grad_attn * attn_norm, axis=0), jnp.sum(grad_mlp * mlp_norm, axis=0)]
        )
        grad_shifts = jnp.stack(
            [
                jnp.sum(grad_attn, axis=0),
                jnp.sum(grad_resid, axis=0),
                jnp.sum(grad_mlp, axis=0),
                jnp.sum(grad_out, axis=0),
            ]
        )
        return (
            grad_in,
            (
                grad_qkv,
                grad_bias,
                grad_outw,
                grad_up,
                jnp.sum(grad_pre, axis=0),
                grad_down,
                grad_gains,
                grad_shifts,
            ),
        )

    def forward_tick(received, tick_index):
        own_at = jnp.minimum(tick_index, groups - 1)
        batch_at = jnp.clip(tick_index - section_index, 0, groups - 1)
        own_in = lax.dynamic_index_in_dim(inputs_all, own_at, 0, keepdims=False)
        layer_in = jnp.where(section_index == 0, own_in, received)
        seq_lengths = lax.dynamic_index_in_dim(lengths, batch_at, 0, keepdims=False)
        layer_out, saved = layer_forward(layer_in, seq_lengths)
        passed = shifted(layer_out.astype(jnp.bfloat16), "pipe", 1)
        return (passed, (layer_out, saved))

    start_rows = jnp.zeros((seq_len, model_width), jnp.bfloat16)
    _, (outputs_all, saves_all) = lax.scan(forward_tick, start_rows, jnp.arange(groups + 1))
    zero_sums = (
        jnp.zeros(qkv_w.shape, jnp.float32),
        jnp.zeros(qv_b.shape, jnp.float32),
        jnp.zeros(out_w.shape, jnp.float32),
        jnp.zeros(up_w.shape, jnp.float32),
        jnp.zeros(up_b.shape, jnp.float32),
        jnp.zeros(down_w.shape, jnp.float32),
        jnp.zeros((2, model_width), jnp.float32),
        jnp.zeros((4, model_width), jnp.float32),
    )

    def backward_tick(carry, tick_index):
        received, running = carry
        source_at = jnp.clip(tick_index + 2 * section_index - 1, 0, groups)
        batch_at = jnp.clip(tick_index + section_index - 1, 0, groups - 1)
        saved = jax.tree.map(
            lambda stacked: lax.dynamic_index_in_dim(stacked, source_at, 0, keepdims=False),
            saves_all,
        )
        own_cot = lax.dynamic_index_in_dim(
            inputs_all, jnp.minimum(tick_index, groups - 1), 0, keepdims=False
        ).astype(jnp.float32)
        live_cot = jnp.where(tick_index < groups, own_cot, jnp.zeros_like(own_cot))
        grad_out = jnp.where(section_index == 1, live_cot, received.astype(jnp.float32))
        seq_lengths = lax.dynamic_index_in_dim(lengths, batch_at, 0, keepdims=False)
        grad_in, terms = layer_backward(grad_out, saved, seq_lengths)
        passed = shifted(grad_in.astype(jnp.bfloat16), "pipe", -1)
        running = tuple((total + term for total, term in zip(running, terms)))
        return ((passed, running), grad_in)

    (_, sums), grads_all = lax.scan(backward_tick, (start_rows, zero_sums), jnp.arange(groups + 1))
    weight_sums = lax.psum((sums[0], sums[1], sums[2], sums[3], sums[4], sums[5]), "dp")
    vector_sums = lax.psum((sums[6], sums[7]), ("tensor", "dp"))
    section_out = jnp.where(section_index == 0, grads_all[1:], outputs_all[1:])[None, :, None]
    return (
        section_out,
        weight_sums[0][None],
        weight_sums[1][None],
        weight_sums[2][None],
        weight_sums[3][None],
        weight_sums[4][None],
        weight_sums[5][None],
        vector_sums[0][None],
        vector_sums[1][None],
    )


def solution(mesh):
    in_specs = (
        P("pipe", "dp", "tensor", None, None),
        P("dp", None),
        P("pipe", None, None, "tensor"),
        P("pipe", None, "tensor"),
        P("pipe", "tensor", None),
        P("pipe", None, "tensor"),
        P("pipe", "tensor"),
        P("pipe", "tensor", None),
        P("pipe", None, None),
        P("pipe", None, None),
    )
    out_specs = (
        P("pipe", "dp", "tensor", None, None),
        P("pipe", None, None, "tensor"),
        P("pipe", None, "tensor"),
        P("pipe", "tensor", None),
        P("pipe", None, "tensor"),
        P("pipe", "tensor"),
        P("pipe", "tensor", None),
        P("pipe", None, None),
        P("pipe", None, None),
    )
    return jax.shard_map(local, mesh=mesh, in_specs=in_specs, out_specs=out_specs, check_vma=False)
```

profile of v0, /device:TPU:0, one launch (start us, length us, event | category | flops | bytes accessed | tf_op | source)
XLA Modules:
  0.0 1544.7 jit_solution(1438076503732215553)
XLA Ops:
  13.6 189.5 %while.63 = (s32[]{:T(128)}, bf16[128,1024]{1,0:T(8,128)(2,1)}, f32[2,128,1024]{2,1,0:T(8,128)}, bf16[2,128,1024]{2,1,0:T(8,128)(2,1)}, bf16[2,3,256,512]{3,2,1,...) while((s32[]{:T(128)}, bf16[128,1024]{1,0:T(8,128)(2,1)}, ...), condition=%wide.region_9.10_spmd.clone.clone, body=%wide.region_0.9_spmd.clone.clone.sunk | while | flops 2227026432 | bytes 96496376 | solution.py:241
  16.5 9.5 all_gather.54
  38.9 25.6 %reduce-scatter.5.cloned.1.call-done = f32[128,1024]{1,0:T(8,128)} async-done(((f32[256,1024]{1,0:T(8,128)}), f32[128,1024]{1,0:T(8,128)}) %reduce-scatter.5.cloned.1.call-update) | async-done | bytes 524304 | tf_op jit(solution)/shard_map/while/body/eval_jaxpr/reduce_scatter | solution.py:126
  67.0 8.8 all_gather.55
  83.3 20.7 %reduce-scatter.7.cloned.1.call-done = f32[128,1024]{1,0:T(8,128)} async-done(((f32[256,1024]{1,0:T(8,128)}), f32[128,1024]{1,0:T(8,128)}) %reduce-scatter.7.cloned.1.call-update) | async-done | bytes 524304 | tf_op jit(solution)/shard_map/while/body/eval_jaxpr/reduce_scatter | solution.py:134
  112.4 8.8 all_gather.54
  134.1 23.9 %reduce-scatter.5.cloned.1.call-done = f32[128,1024]{1,0:T(8,128)} async-done(((f32[256,1024]{1,0:T(8,128)}), f32[128,1024]{1,0:T(8,128)}) %reduce-scatter.5.cloned.1.call-update) | async-done | bytes 524304 | tf_op jit(solution)/shard_map/while/body/eval_jaxpr/reduce_scatter | solution.py:126
  160.5 8.8 all_gather.55
  176.8 20.7 %reduce-scatter.7.cloned.1.call-done = f32[128,1024]{1,0:T(8,128)} async-done(((f32[256,1024]{1,0:T(8,128)}), f32[128,1024]{1,0:T(8,128)}) %reduce-scatter.7.cloned.1.call-update) | async-done | bytes 524304 | tf_op jit(solution)/shard_map/while/body/eval_jaxpr/reduce_scatter | solution.py:134
  205.5 253.4 %while.64 = (s32[]{:T(128)}, bf16[128,1024]{1,0:T(8,128)(2,1)}, f32[3,1024,512]{1,2,0:T(8,128)}, f32[2,512]{1,0:T(2,128)}, f32[512,1024]{1,0:T(8,128)}, /*index=...) while((s32[]{:T(128)}, bf16[128,1024]{1,0:T(8,128)(2,1)}, ...), condition=%wide.region_31.32_spmd.clone.clone, body=%wide.region_10.31_spmd.clone.clone.sunk | while | flops 4491193856 | bytes 120951592 | solution.py:272
  209.1 7.9 all_gather.56
  216.9 4.2 fusion.236
  251.9 8.7 all_gather.57
  280.5 3.9 convolution_bitcast_fusion.4
  285.7 4.0 select_add_fusion.11
  289.8 11.6 all_gather.59
  315.1 9.0 all_gather.58
  324.2 3.7 bitcast_add_fusion.2
  332.1 9.5 all_gather.56
  341.7 4.2 fusion.236
  376.7 8.7 all_gather.57
  405.3 3.9 convolution_bitcast_fusion.4
  410.4 5.3 select_add_fusion.11
  415.9 13.3 all_gather.59
  429.2 3.5 select_add_fusion.8
  432.7 5.1 select_add_fusion.9
  442.7 9.0 all_gather.58
  451.7 6.6 bitcast_add_fusion.2
  458.9 6.6 copy.63
  466.2 104.3 %all-reduce.1 = (f32[1,2,512]{2,1,0:T(2,128)}, f32[1,1024]{1,0:T(1,128)}) all-reduce(f32[1,2,512]{2,1,0:T(2,128)S(1)} %bitcast.394, f32[1,1024]{1,0:T(1,128)S(1)} %bitcast.393), channel_id=1, replica_groups=mesh['pipe'=2,'tensor'=2,'dp'=32] {'dp'}, use_global_device_ids=true, to_apply=%region_33.34 | all-reduce | flops 2048 | bytes 16384 | tf_op jit(solution)/shard_map/psum | solution.py:273
  570.6 950.9 %all-reduce = (f32[1,2,1024]{2,1,0:T(2,128)}, f32[1,4,1024]{2,1,0:T(4,128)}) all-reduce(f32[1,2,1024]{2,1,0:T(2,128)S(1)} %bitcast.392, f32[1,4,1024]{2,1,0:T(4,128)S(1)} %bitcast.377), channel_id=1, replica_groups=mesh['pipe'=2,'tensor'=2,'dp'=32] {'tensor','dp'}, use_global_device_ids=true, to_apply=%region_38.39 | all-reduce | flops 6144 | bytes 49152 | tf_op jit(solution)/shard_map/psum | solution.py:274
  1522.3 6.3 copy.215
  (407 shorter events, 208.4 us)
Async XLA Ops:
  13.6 50.9 %reduce-scatter.5.cloned.1.call-start = ((), (), s32[]{:S(2)}) async-start(), calls=%async_computation.5 | async-start | bytes 1572864 | tf_op jit(solution)/shard_map/while/body/eval_jaxpr/reduce_scatter | solution.py:126
  13.7 12.3 copy-start.15
  13.7 12.3 copy-start.41
  38.9 65.1 %reduce-scatter.7.cloned.1.call-start = ((), (), s32[]{:S(2)}) async-start(), calls=%async_computation.6 | async-start | bytes 1572864 | tf_op jit(solution)/shard_map/while/body/eval_jaxpr/reduce_scatter | solution.py:134
  66.6 9.2 copy-start.43
  80.9 28.6 %copy-start.39 = (f32[2,2,8,128,1]{3,2,1,4,0:T(8,128)}, f32[2,2,8,128,1]{3,2,1,4,0:T(8,128)S(1)}, u32[]{:S(2)}) copy-start(f32[2,2,8,128,1]{3,2,1,4,0:T(8,128)S(1)} %bitcast_dynamic-update-slice_fusion.21) | copy-start | bytes 49156 | tf_op jit(solution)/shard_map/while
  105.1 4.4 collective-permute-start
  109.5 48.5 %reduce-scatter.5.cloned.1.call-start = ((), (), s32[]{:S(2)}) async-start(), calls=%async_computation.5 | async-start | bytes 1572864 | tf_op jit(solution)/shard_map/while/body/eval_jaxpr/reduce_scatter | solution.py:126
  109.6 11.6 copy-start.15
  109.6 11.6 copy-start.41
  134.0 63.5 %reduce-scatter.7.cloned.1.call-start = ((), (), s32[]{:S(2)}) async-start(), calls=%async_computation.6 | async-start | bytes 1572864 | tf_op jit(solution)/shard_map/while/body/eval_jaxpr/reduce_scatter | solution.py:134
  160.1 9.3 copy-start.43
  174.5 28.6 %copy-start.39 = (f32[2,2,8,128,1]{3,2,1,4,0:T(8,128)}, f32[2,2,8,128,1]{3,2,1,4,0:T(8,128)S(1)}, u32[]{:S(2)}) copy-start(f32[2,2,8,128,1]{3,2,1,4,0:T(8,128)S(1)} %bitcast_dynamic-update-slice_fusion.21) | copy-start | bytes 49156 | tf_op jit(solution)/shard_map/while
  198.6 4.4 collective-permute-start
  205.5 44.1 %copy-start.8 = (bf16[1,128,1024]{2,1,0:T(8,128)(2,1)}, bf16[1,128,1024]{2,1,0:T(8,128)(2,1)S(1)}, u32[]{:S(2)}) copy-start(bf16[1,128,1024]{2,1,0:T(8,128)(2,1)S(1)} %get-tuple-element.1786) | copy-start | bytes 786436 | tf_op jit(solution)/shard_map/while
  205.5 42.1 %reduce-scatter.9.cloned.1.call-start = ((), (), s32[]{:S(2)}) async-start(), calls=%async_computation.7 | async-start | bytes 1572864 | tf_op jit(solution)/shard_map/while/body/eval_jaxpr/reduce_scatter | solution.py:158
  223.6 86.6 %reduce-scatter.11.cloned.1.call-start = ((), (), s32[]{:S(2)}) async-start(), calls=%async_computation.8 | async-start | bytes 1572864 | tf_op jit(solution)/shard_map/while/body/eval_jaxpr/reduce_scatter | solution.py:201
  249.6 11.1 copy-start.6
  261.8 7.6 copy-start.13
  285.7 15.7 %copy-start.31 = (f32[2,512]{1,0:T(2,128)S(1)}, f32[2,512]{1,0:T(2,128)}, u32[]{:S(2)}) copy-start(f32[2,512]{1,0:T(2,128)} %get-tuple-element.1741) | copy-start | bytes 12292 | tf_op jit(solution)/shard_map/while
  313.9 14.1 collective-permute-start.1
  328.5 45.8 %copy-start.8 = (bf16[1,128,1024]{2,1,0:T(8,128)(2,1)}, bf16[1,128,1024]{2,1,0:T(8,128)(2,1)S(1)}, u32[]{:S(2)}) copy-start(bf16[1,128,1024]{2,1,0:T(8,128)(2,1)S(1)} %get-tuple-element.1786) | copy-start | bytes 786436 | tf_op jit(solution)/shard_map/while
  328.5 43.8 %reduce-scatter.9.cloned.1.call-start = ((), (), s32[]{:S(2)}) async-start(), calls=%async_computation.7 | async-start | bytes 1572864 | tf_op jit(solution)/shard_map/while/body/eval_jaxpr/reduce_scatter | solution.py:158
  348.4 89.4 %reduce-scatter.11.cloned.1.call-start = ((), (), s32[]{:S(2)}) async-start(), calls=%async_computation.8 | async-start | bytes 1572864 | tf_op jit(solution)/shard_map/while/body/eval_jaxpr/reduce_scatter | solution.py:201
  374.3 11.1 copy-start.6
  386.5 7.5 copy-start.13
  410.4 18.7 %copy-start.31 = (f32[2,512]{1,0:T(2,128)S(1)}, f32[2,512]{1,0:T(2,128)}, u32[]{:S(2)}) copy-start(f32[2,512]{1,0:T(2,128)} %get-tuple-element.1741) | copy-start | bytes 12292 | tf_op jit(solution)/shard_map/while
  441.4 17.0 %collective-permute-start.1 = (bf16[128,1024]{1,0:T(8,128)(2,1)S(1)}, bf16[128,1024]{1,0:T(8,128)(2,1)}, u32[]{:S(2)}, u32[]{:S(2)}) collective-permute-start(bf16[128,1024]{1,0:T(8,128)(2,1)S(1)} %get-tuple-element.1618), channel_id=1, source_target_pairs={{64,0},{65,1},{66,2},{67,3},{68,4},{69,5},{70,6},{71,7},{72,8},{73... | collective-permute-start | bytes 786440 | tf_op jit(solution)/shard_map/while/body/eval_jaxpr/ppermute | solution.py:14
  458.9 1063.4 %all-reduce.5.cloned.1.call-start = ((), (), s32[]{:S(2)}) async-start(), calls=%async_computation.4 | async-start | bytes 33554432 | tf_op jit(solution)/shard_map/psum | solution.py:273
  465.5 105.0 %copy-start.27 = (f32[2,1024]{1,0:T(2,128)S(1)}, f32[2,1024]{1,0:T(2,128)}, u32[]{:S(2)}) copy-start(f32[2,1024]{1,0:T(2,128)} %get-tuple-element.751) | copy-start | bytes 24580
  465.5 1055.9 %copy-start.20 = (f32[2,128,1024]{2,1,0:T(8,128)S(1)}, f32[2,128,1024]{2,1,0:T(8,128)}, u32[]{:S(2)}) copy-start(f32[2,128,1024]{2,1,0:T(8,128)} %get-tuple-element.743) | copy-start | bytes 3145732
  465.5 1055.9 %copy-start.21 = (f32[2,128,1024]{2,1,0:T(8,128)S(1)}, f32[2,128,1024]{2,1,0:T(8,128)}, u32[]{:S(2)}) copy-start(f32[2,128,1024]{2,1,0:T(8,128)} %get-tuple-element.744) | copy-start | bytes 3145732
  (59 other events, 195.8 us)
Sparse Core Ops, SparseCore 0:
  39.0 25.4 reduce-scatter.4
  80.1 23.8 reduce-scatter.6
  134.2 23.7 reduce-scatter.4
  173.7 23.8 reduce-scatter.6
  223.7 23.7 reduce-scatter.8
  284.6 25.6 reduce-scatter.10
  348.5 23.7 reduce-scatter.8
  409.3 26.9 reduce-scatter.10
Sparse Core Ops, SparseCore 1:
  465.6 743.7 all-reduce.4
where the time goes:
time: 1550 us; the launch traced here: 1540 us
  blocking collectives  1170 us (75%)
  waiting for transfers between devices  99.9 us (6%)
  local copies, waits for them, and re-layouts  99 us (6%)
  matrix products  98.1 us (6%)
  other arithmetic  51.6 us (3%)
  between operations  15.6 us (1%)
    psum x1, blocking collectives, local(): vector_sums = lax.psum((sums[6], sums[7]), ('tensor', 'dp'))  951 us
    psum x1, blocking collectives, local(): lax.psum((sums[0], sums[1], sums[2], sums[3], sums[4], sums[5]), 'dp')  104 us
    reduce_scatter x2, waiting for transfers between devices, layer_forward(): lax.psum_scatter(rows_product(context, out_w, 'rw,wd->rd'), 'tensor', sca...  49.5 us
    reduce_scatter x2, waiting for transfers between devices, layer_forward(): lax.psum_scatter(rows_product(activated, down_w, 'rf,fd->rd'), 'tensor',...  41.4 us
    squeeze x18, local copies, waits for them, and re-layouts, split_heads(): return block.reshape(tensor_size, seq_len, heads_dev, HD)  31.4 us
  transfers between devices with their start and end apart: 13, of which 7 were waited for; matrix products, arithmetic and copies ran while one was open for 6% of the time, Pallas kernels for 0%

commit v1 on v0

--- a/solution.py
+++ b/solution.py
@@ -271,7 +271,7 @@
 
     (_, sums), grads_all = lax.scan(backward_tick, (start_rows, zero_sums), jnp.arange(groups + 1))
     weight_sums = lax.psum((sums[0], sums[1], sums[2], sums[3], sums[4], sums[5]), "dp")
-    vector_sums = lax.psum((sums[6], sums[7]), ("tensor", "dp"))
+    vector_sums = lax.psum(lax.psum((sums[6], sums[7]), "tensor"), "dp")
     section_out = jnp.where(section_index == 0, grads_all[1:], outputs_all[1:])[None, :, None]
     return (
         section_out,

time: 1550 us -> 1230 us (0.79)
  blocking collectives: 1170 us -> 315 us
  waiting for transfers between devices: 99.9 us -> 640 us
    psum x1, blocking collectives: 951 us -> 7.03 us  [local(): vector_sums = lax.psum(lax.psum((sums[6], sums[7]), 'tensor'), 'dp')]
    psum x1, waiting for transfers between devices: 0.01 us -> 540 us  [local(): lax.psum((sums[0], sums[1], sums[2], sums[3], sums[4], sums[5]), 'dp')]
    psum x1, blocking collectives: 104 us -> 194 us  [local(): lax.psum((sums[0], sums[1], sums[2], sums[3], sums[4], sums[5]), 'dp')]
  transfers between devices with their start and end apart: 13 -> 13, of which waited for: 7 -> 8; matrix products, arithmetic and copies ran while one was open for 6% -> 7% of each run, Pallas kernels for 0% -> 0%
where the time goes in v1:
time: 1230 us
  waiting for transfers between devices  640 us (52%)
  blocking collectives  315 us (26%)
  local copies, waits for them, and re-layouts  99 us (8%)
  matrix products  98.1 us (8%)
  other arithmetic  51.6 us (4%)
  between operations  15.7 us (1%)
    psum x1, waiting for transfers between devices, local(): lax.psum((sums[0], sums[1], sums[2], sums[3], sums[4], sums[5]), 'dp')  540 us
    psum x1, blocking collectives, local(): lax.psum((sums[0], sums[1], sums[2], sums[3], sums[4], sums[5]), 'dp')  194 us
    reduce_scatter x2, waiting for transfers between devices, layer_forward(): lax.psum_scatter(rows_product(context, out_w, 'rw,wd->rd'), 'tensor', sca...  49.5 us
    reduce_scatter x2, waiting for transfers between devices, layer_forward(): lax.psum_scatter(rows_product(activated, down_w, 'rf,fd->rd'), 'tensor',...  41.4 us
    squeeze x18, local copies, waits for them, and re-layouts, split_heads(): return block.reshape(tensor_size, seq_len, heads_dev, HD)  31.4 us
    all_gather x2, blocking collectives, layer_backward(): lax.all_gather(mlp_f.astype(jnp.bfloat16), 'tensor', axis=0, tiled=True)  24.9 us
  transfers between devices with their start and end apart: 13, of which 8 were waited for; matrix products, arithmetic and copies ran while one was open for 7% of the time, Pallas kernels for 0%

profile of v1, /device:TPU:0, one launch (start us, length us, event | category | flops | bytes accessed | tf_op | source)
XLA Modules:
  0.0 1230.5 jit_solution(11006682290865692937)
XLA Ops:
  13.6 189.5 %while.63 = (s32[]{:T(128)}, bf16[128,1024]{1,0:T(8,128)(2,1)}, f32[2,128,1024]{2,1,0:T(8,128)}, bf16[2,128,1024]{2,1,0:T(8,128)(2,1)}, bf16[2,3,256,512]{3,2,1,...) while((s32[]{:T(128)}, bf16[128,1024]{1,0:T(8,128)(2,1)}, ...), condition=%wide.region_9.10_spmd.clone.clone, body=%wide.region_0.9_spmd.clone.clone.sunk | while | flops 2227026432 | bytes 96496376 | solution.py:241
  16.5 9.5 all_gather.54
  38.9 25.6 %reduce-scatter.5.cloned.1.call-done = f32[128,1024]{1,0:T(8,128)} async-done(((f32[256,1024]{1,0:T(8,128)}), f32[128,1024]{1,0:T(8,128)}) %reduce-scatter.5.cloned.1.call-update) | async-done | bytes 524304 | tf_op jit(solution)/shard_map/while/body/eval_jaxpr/reduce_scatter | solution.py:126
  67.0 8.8 all_gather.55
  83.3 20.7 %reduce-scatter.7.cloned.1.call-done = f32[128,1024]{1,0:T(8,128)} async-done(((f32[256,1024]{1,0:T(8,128)}), f32[128,1024]{1,0:T(8,128)}) %reduce-scatter.7.cloned.1.call-update) | async-done | bytes 524304 | tf_op jit(solution)/shard_map/while/body/eval_jaxpr/reduce_scatter | solution.py:134
  112.4 8.8 all_gather.54
  134.1 23.9 %reduce-scatter.5.cloned.1.call-done = f32[128,1024]{1,0:T(8,128)} async-done(((f32[256,1024]{1,0:T(8,128)}), f32[128,1024]{1,0:T(8,128)}) %reduce-scatter.5.cloned.1.call-update) | async-done | bytes 524304 | tf_op jit(solution)/shard_map/while/body/eval_jaxpr/reduce_scatter | solution.py:126
  160.5 8.8 all_gather.55
  176.8 20.7 %reduce-scatter.7.cloned.1.call-done = f32[128,1024]{1,0:T(8,128)} async-done(((f32[256,1024]{1,0:T(8,128)}), f32[128,1024]{1,0:T(8,128)}) %reduce-scatter.7.cloned.1.call-update) | async-done | bytes 524304 | tf_op jit(solution)/shard_map/while/body/eval_jaxpr/reduce_scatter | solution.py:134
  205.5 253.4 %while.64 = (s32[]{:T(128)}, bf16[128,1024]{1,0:T(8,128)(2,1)}, f32[3,1024,512]{1,2,0:T(8,128)}, f32[2,512]{1,0:T(2,128)}, f32[512,1024]{1,0:T(8,128)}, /*index=...) while((s32[]{:T(128)}, bf16[128,1024]{1,0:T(8,128)(2,1)}, ...), condition=%wide.region_31.32_spmd.clone.clone, body=%wide.region_10.31_spmd.clone.clone.sunk | while | flops 4491193856 | bytes 120951592 | solution.py:272
  209.1 7.9 all_gather.56
  216.9 4.2 fusion.236
  251.9 8.7 all_gather.57
  280.5 3.9 convolution_bitcast_fusion.4
  285.7 4.0 select_add_fusion.11
  289.8 11.6 all_gather.59
  315.1 9.0 all_gather.58
  324.2 3.7 bitcast_add_fusion.2
  332.1 9.5 all_gather.56
  341.7 4.2 fusion.236
  376.7 8.7 all_gather.57
  405.3 3.9 convolution_bitcast_fusion.4
  410.4 5.3 select_add_fusion.11
  415.9 13.3 %all_gather.59 = bf16[256,1024]{1,0:T(8,128)(2,1)S(1)} all-gather(bf16[128,1024]{1,0:T(8,128)(2,1)} %get-tuple-element.1624), channel_id=1, replica_groups=mesh['pipe'=2,'tensor'=2,'dp'=32] {'tensor'}, dimensions={0}, use_global_device_ids=true | all-gather | bytes 786432 | tf_op jit(solution)/shard_map/while/body/eval_jaxpr/all_gather | solution.py:145
  432.7 5.1 select_add_fusion.9
  442.7 9.0 all_gather.58
  451.7 6.6 bitcast_add_fusion.2
  458.9 6.6 copy.63
  466.2 7.0 all-reduce.2
  473.3 193.9 %all-reduce = (f32[1,2,512]{2,1,0:T(2,128)}, f32[1,1024]{1,0:T(1,128)}, f32[1,2,1024]{2,1,0:T(2,128)}, f32[1,4,1024]{2,1,0:T(4,128)}) all-reduce(f32[1,2,512]{2,1,0:T(2,128)S(1)} %bitcast.392, f32[1,1024]{1,0:T(1,128)S(1)} %bitcast.391, f32[1,2,1024]{2,1,0:T(2,128)S(1)} %bitcast.395, ...), channel_id=1, replica_groups=mesh['pipe'=2,'tensor'=2,'dp'=32] {'dp'}, use_global_device_ids=true, to_apply=%region_33.34 | all-reduce | flops 8192 | bytes 65536 | tf_op jit(solution)/shard_map/psum | solution.py:273
  668.0 540.0 %all-reduce.5.cloned.1.call-done = (f32[1,3,1024,512]{3,2,1,0:T(8,128)}, f32[1,512,1024]{2,1,0:T(8,128)}, f32[1,1024,1024]{2,1,0:T(8,128)}, f32[1,1024,1024]{2,1,0:T(8,128)}) async-done(((f32[1,3,1024,512]{3,2,1,0:T(8,128)}, f32[1,512,1024]{2,1,0:T(8,128)}, f32[1,1024,1024]{2,1,0:T(8,128)}, f32[1,1024,1024]{2,1,0:T(8,128)}), (f32[1,3,1024,512]{3,2,1,0:T(8,128)}, f32[1,512,1024]{2,1,0:T(8,128)}, ...) | async-done | bytes 16777232 | tf_op jit(solution)/shard_map/psum | solution.py:273
  1208.0 6.3 copy.215
  (407 shorter events, 211.9 us)
Async XLA Ops:
  13.6 50.9 %reduce-scatter.5.cloned.1.call-start = ((), (), s32[]{:S(2)}) async-start(), calls=%async_computation.5 | async-start | bytes 1572864 | tf_op jit(solution)/shard_map/while/body/eval_jaxpr/reduce_scatter | solution.py:126
  13.7 12.3 %copy-start.15 = (bf16[2,3,256,512]{3,2,1,0:T(8,128)(2,1)S(1)}, bf16[2,3,256,512]{3,2,1,0:T(8,128)(2,1)}, u32[]{:S(2)}) copy-start(bf16[2,3,256,512]{3,2,1,0:T(8,128)(2,1)} %get-tuple-element.1661) | copy-start | bytes 4718596 | tf_op jit(solution)/shard_map/while
  13.7 12.3 %copy-start.41 = (f32[3,1,512]{2,0,1:T(4,128)S(1)}, f32[3,1,512]{2,0,1:T(4,128)}, u32[]{:S(2)}) copy-start(f32[3,1,512]{2,0,1:T(4,128)} %get-tuple-element.1696) | copy-start | bytes 18436 | tf_op jit(solution)/shard_map/while
  38.9 65.1 %reduce-scatter.7.cloned.1.call-start = ((), (), s32[]{:S(2)}) async-start(), calls=%async_computation.6 | async-start | bytes 1572864 | tf_op jit(solution)/shard_map/while/body/eval_jaxpr/reduce_scatter | solution.py:134
  66.6 9.2 copy-start.43
  80.9 28.6 %copy-start.39 = (f32[2,2,8,128,1]{3,2,1,4,0:T(8,128)}, f32[2,2,8,128,1]{3,2,1,4,0:T(8,128)S(1)}, u32[]{:S(2)}) copy-start(f32[2,2,8,128,1]{3,2,1,4,0:T(8,128)S(1)} %bitcast_dynamic-update-slice_fusion.21) | copy-start | bytes 49156 | tf_op jit(solution)/shard_map/while
  105.1 4.4 collective-permute-start
  109.5 48.5 %reduce-scatter.5.cloned.1.call-start = ((), (), s32[]{:S(2)}) async-start(), calls=%async_computation.5 | async-start | bytes 1572864 | tf_op jit(solution)/shard_map/while/body/eval_jaxpr/reduce_scatter | solution.py:126
  109.6 11.6 copy-start.15
  109.6 11.6 copy-start.41
  134.0 63.5 %reduce-scatter.7.cloned.1.call-start = ((), (), s32[]{:S(2)}) async-start(), calls=%async_computation.6 | async-start | bytes 1572864 | tf_op jit(solution)/shard_map/while/body/eval_jaxpr/reduce_scatter | solution.py:134
  160.1 9.3 copy-start.43
  174.5 28.6 %copy-start.39 = (f32[2,2,8,128,1]{3,2,1,4,0:T(8,128)}, f32[2,2,8,128,1]{3,2,1,4,0:T(8,128)S(1)}, u32[]{:S(2)}) copy-start(f32[2,2,8,128,1]{3,2,1,4,0:T(8,128)S(1)} %bitcast_dynamic-update-slice_fusion.21) | copy-start | bytes 49156 | tf_op jit(solution)/shard_map/while
  198.6 4.4 collective-permute-start
  205.5 44.1 %copy-start.8 = (bf16[1,128,1024]{2,1,0:T(8,128)(2,1)}, bf16[1,128,1024]{2,1,0:T(8,128)(2,1)S(1)}, u32[]{:S(2)}) copy-start(bf16[1,128,1024]{2,1,0:T(8,128)(2,1)S(1)} %get-tuple-element.1788) | copy-start | bytes 786436 | tf_op jit(solution)/shard_map/while
  205.5 42.1 %reduce-scatter.9.cloned.1.call-start = ((), (), s32[]{:S(2)}) async-start(), calls=%async_computation.7 | async-start | bytes 1572864 | tf_op jit(solution)/shard_map/while/body/eval_jaxpr/reduce_scatter | solution.py:158
  223.6 86.6 %reduce-scatter.11.cloned.1.call-start = ((), (), s32[]{:S(2)}) async-start(), calls=%async_computation.8 | async-start | bytes 1572864 | tf_op jit(solution)/shard_map/while/body/eval_jaxpr/reduce_scatter | solution.py:201
  249.6 11.1 copy-start.6
  261.8 7.6 copy-start.13
  285.7 15.7 %copy-start.31 = (f32[2,512]{1,0:T(2,128)S(1)}, f32[2,512]{1,0:T(2,128)}, u32[]{:S(2)}) copy-start(f32[2,512]{1,0:T(2,128)} %get-tuple-element.1743) | copy-start | bytes 12292 | tf_op jit(solution)/shard_map/while
  313.9 14.1 %collective-permute-start.1 = (bf16[128,1024]{1,0:T(8,128)(2,1)S(1)}, bf16[128,1024]{1,0:T(8,128)(2,1)}, u32[]{:S(2)}, u32[]{:S(2)}) collective-permute-start(bf16[128,1024]{1,0:T(8,128)(2,1)S(1)} %get-tuple-element.1620), channel_id=1, source_target_pairs={{64,0},{65,1},{66,2},{67,3},{68,4},{69,5},{70,6},{71,7},{72,8},{73... | collective-permute-start | bytes 786440 | tf_op jit(solution)/shard_map/while/body/eval_jaxpr/ppermute | solution.py:14
  328.5 45.8 %copy-start.8 = (bf16[1,128,1024]{2,1,0:T(8,128)(2,1)}, bf16[1,128,1024]{2,1,0:T(8,128)(2,1)S(1)}, u32[]{:S(2)}) copy-start(bf16[1,128,1024]{2,1,0:T(8,128)(2,1)S(1)} %get-tuple-element.1788) | copy-start | bytes 786436 | tf_op jit(solution)/shard_map/while
  328.5 43.8 %reduce-scatter.9.cloned.1.call-start = ((), (), s32[]{:S(2)}) async-start(), calls=%async_computation.7 | async-start | bytes 1572864 | tf_op jit(solution)/shard_map/while/body/eval_jaxpr/reduce_scatter | solution.py:158
  348.4 89.4 %reduce-scatter.11.cloned.1.call-start = ((), (), s32[]{:S(2)}) async-start(), calls=%async_computation.8 | async-start | bytes 1572864 | tf_op jit(solution)/shard_map/while/body/eval_jaxpr/reduce_scatter | solution.py:201
  374.3 11.1 copy-start.6
  410.4 18.7 %copy-start.31 = (f32[2,512]{1,0:T(2,128)S(1)}, f32[2,512]{1,0:T(2,128)}, u32[]{:S(2)}) copy-start(f32[2,512]{1,0:T(2,128)} %get-tuple-element.1743) | copy-start | bytes 12292 | tf_op jit(solution)/shard_map/while
  441.4 17.0 %collective-permute-start.1 = (bf16[128,1024]{1,0:T(8,128)(2,1)S(1)}, bf16[128,1024]{1,0:T(8,128)(2,1)}, u32[]{:S(2)}, u32[]{:S(2)}) collective-permute-start(bf16[128,1024]{1,0:T(8,128)(2,1)S(1)} %get-tuple-element.1620), channel_id=1, source_target_pairs={{64,0},{65,1},{66,2},{67,3},{68,4},{69,5},{70,6},{71,7},{72,8},{73... | collective-permute-start | bytes 786440 | tf_op jit(solution)/shard_map/while/body/eval_jaxpr/ppermute | solution.py:14
  458.9 749.1 %all-reduce.5.cloned.1.call-start = ((), (), s32[]{:S(2)}) async-start(), calls=%async_computation.4 | async-start | bytes 33554432 | tf_op jit(solution)/shard_map/psum | solution.py:273
  465.5 7.7 copy-start.30
  465.5 7.7 copy-start.33
  465.5 201.6 %copy-start.20 = (f32[2,128,1024]{2,1,0:T(8,128)S(1)}, f32[2,128,1024]{2,1,0:T(8,128)}, u32[]{:S(2)}) copy-start(f32[2,128,1024]{2,1,0:T(8,128)} %get-tuple-element.743) | copy-start | bytes 3145732
  465.5 201.6 %copy-start.21 = (f32[2,128,1024]{2,1,0:T(8,128)S(1)}, f32[2,128,1024]{2,1,0:T(8,128)}, u32[]{:S(2)}) copy-start(f32[2,128,1024]{2,1,0:T(8,128)} %get-tuple-element.744) | copy-start | bytes 3145732
  (59 other events, 202.6 us)
Sparse Core Ops, SparseCore 0:
  39.0 25.4 reduce-scatter.4
  80.1 23.8 reduce-scatter.6
  134.2 23.7 reduce-scatter.4
  173.7 23.8 reduce-scatter.6
  223.7 23.7 reduce-scatter.8
  284.6 25.6 reduce-scatter.10
  348.5 23.7 reduce-scatter.8
  409.3 26.9 reduce-scatter.10
Sparse Core Ops, SparseCore 1:
  465.6 742.3 all-reduce.4
